TPU v7x, 512 devices: a whole 4x8x8 slice. The times are simulated.
512 devices in a mesh: dp: 32 (over x, y), table: 16 (over z, core).
Axes of the slice: x: 4, y: 8, z: 8, core: 2. Of those that a mesh axis runs over, the one named last changes fastest.
Arguments:
- table: bfloat16 [12288, 512], P('table'), may hold values from -6 to 6
- history_shard: int32 [512, 256, 1], P(('dp', 'table')), may hold values from 0 to 15; in each aligned block of 256 rows (0 to 255, 256 to 511, ..., all dimensions but the last counted through in order) at most 32 rows name the same one
- history_row: int32 [512, 256], P(('dp', 'table')), may hold values from 0 to 767
- lengths: int32 [512], P(('dp', 'table')), may hold values from 1 to 256, 98304 in all
- w_in: bfloat16 [512, 2048], replicated, may hold values from -0.25 to 0.25
- w_out: bfloat16 [512, 512], replicated, may hold values from -0.25 to 0.25
- cotangent: bfloat16 [512, 256, 512], P(('dp', 'table')), may hold values from -6 to 6
Outputs:
- table_grad: float32 [12288, 512], P('table')
- dense_grad: bfloat16 [512, 512], replicated
Inputs may be any that keep to these rules, and one draw needn't show every extreme that they name: `history_shard`: among the 256 history slots of one device's samples, at most 32 name one table shard, and that bound is met by some shard in some device's slots. `lengths`: some sample has the full length 256.
All inputs are finite; a program needn't handle non-finite values. No bound on the sum of `lengths` on one device may be relied on, other than what follows from the above.
Results may differ from a plain program's by a relative error of at most 0.017.
Values may be sent and summed in bfloat16 or wider, within the bound.
A program may use at most 64 MiB of HBM per device.

v0:
```python
import math
import jax
import jax.numpy as jnp
from jax import lax
from jax.sharding import PartitionSpec as P

HEADS = 4


def layer_norm(values):
    average = jnp.mean(values, axis=-1, keepdims=True)
    centred = values - average
    variance = jnp.mean(centred * centred, axis=-1, keepdims=True)
    return centred * lax.rsqrt(variance + 1e-06)


def hstu_layer(embedded, w_in, w_out, lengths):
    samples_here, seq_span, model_width = embedded.shape
    head_dim = model_width // HEADS
    normed = layer_norm(embedded.astype(jnp.float32)).astype(jnp.bfloat16)
    projected = jax.nn.silu(
        jnp.dot(
            normed.reshape(samples_here * seq_span, model_width),
            w_in,
            preferred_element_type=jnp.float32,
        )
    )
    gate_part = projected[:, :model_width]
    shaped = (samples_here, seq_span, HEADS, head_dim)
    values = projected[:, model_width : 2 * model_width].astype(jnp.bfloat16).reshape(shaped)
    queries = projected[:, 2 * model_width : 3 * model_width].astype(jnp.bfloat16).reshape(shaped)
    keys = projected[:, 3 * model_width :].astype(jnp.bfloat16).reshape(shaped)
    scores = jnp.einsum(
        "blhd,bmhd->bhlm", queries.astype(jnp.float32), keys.astype(jnp.float32)
    ) * head_dim ** (-0.5)
    positions = jnp.arange(seq_span)
    live_keys = (positions[None, None, :] <= positions[None, :, None]) & (
        positions[None, None, :] < lengths[:, None, None]
    )
    weights = (
        jnp.where(live_keys[:, None], jax.nn.silu(scores), 0.0)
        / lengths.astype(jnp.float32)[:, None, None, None]
    )
    weights = weights.astype(jnp.bfloat16)
    attended = jnp.einsum(
        "bhlm,bmhd->blhd", weights.astype(jnp.float32), values.astype(jnp.float32)
    ).reshape(samples_here * seq_span, model_width)
    mixed = (layer_norm(attended) * gate_part).astype(jnp.bfloat16)
    output = jnp.dot(mixed, w_out, preferred_element_type=jnp.float32) + embedded.reshape(
        -1, model_width
    ).astype(jnp.float32)
    return (output, mixed)


def per_device(table, history_shard, history_row, lengths, w_in, w_out, cotangent):
    shard_rows, model_width = table.shape
    samples_here, seq_span = history_row.shape
    groups = lax.axis_size("table")
    slot_count = samples_here * seq_span
    capacity = 2 * slot_count // groups
    owners = history_shard[:, :, 0].reshape(-1)
    local_rows = history_row.reshape(-1)
    owner_hits = (owners[:, None] == jnp.arange(groups)[None, :]).astype(jnp.int32)
    slot_rank = jnp.sum((jnp.cumsum(owner_hits, axis=0) - owner_hits) * owner_hits, axis=1)
    position = owners * capacity + slot_rank
    requested = (
        jnp.zeros((groups * capacity,), jnp.int32)
        .at[position]
        .set(local_rows)
        .reshape(groups, capacity)
    )
    incoming = lax.all_to_all(requested, "table", split_axis=0, concat_axis=0, tiled=True).reshape(
        -1
    )
    global_rows = owners * shard_rows + local_rows
    piece = lax.all_gather(table, "table", axis=0, tiled=True)
    inside = (global_rows >= 0) & (global_rows < piece.shape[0])
    taken = piece[jnp.clip(global_rows, 0, piece.shape[0] - 1)].astype(jnp.float32)
    embedded = jnp.where(inside[:, None], taken, 0.0).astype(jnp.bfloat16)
    embedded = embedded.reshape(samples_here, seq_span, model_width)
    output, pullback, mixed = jax.vjp(
        lambda rows_in: hstu_layer(rows_in, w_in, w_out, lengths), embedded, has_aux=True
    )
    row_live = jnp.arange(seq_span)[None, :] < lengths[:, None]
    grad_seed = jnp.where(row_live[:, :, None], cotangent, jnp.zeros_like(cotangent))
    flat_seed = grad_seed.reshape(-1, model_width)
    (row_grad,) = pullback(flat_seed.astype(jnp.float32))
    dense_part = jnp.dot(mixed.T, flat_seed, preferred_element_type=jnp.float32)
    outgoing = (
        jnp.zeros((groups * capacity, model_width), jnp.bfloat16)
        .at[position]
        .set(row_grad.reshape(-1, model_width))
    )
    arrived = lax.all_to_all(
        outgoing.reshape(groups, capacity, model_width),
        "table",
        split_axis=0,
        concat_axis=0,
        tiled=True,
    )
    local_grad = (
        jnp.zeros((shard_rows, model_width), jnp.float32)
        .at[incoming]
        .add(arrived.reshape(-1, model_width).astype(jnp.float32))
    )
    total_slots = slot_count * lax.axis_size("dp") * groups
    grad_scale = 1.0 / math.sqrt(total_slots)
    table_grad = lax.psum(local_grad, "dp")
    dense_total = lax.psum(dense_part, ("dp", "table"))
    dense_grad = (dense_total * grad_scale).astype(jnp.bfloat16)
    return (table_grad, dense_grad)


def solution(mesh):
    in_specs = (
        P("table", None),
        P(("dp", "table"), None, None),
        P(("dp", "table"), None),
        P(("dp", "table")),
        P(),
        P(),
        P(("dp", "table"), None, None),
    )
    out_specs = (P("table", None), P())
    return jax.shard_map(
        per_device, mesh=mesh, in_specs=in_specs, out_specs=out_specs, check_vma=False
    )
```

profile of v0, /device:TPU:64, one launch (start us, length us, event | category | flops | bytes accessed | tf_op | source)
XLA Modules:
  0.0 582.9 jit_solution(10138484838293075610)
XLA Ops:
  7.2 0.0 copy-start
  7.2 0.0 all-gather.2.cloned.1.call-start
  7.2 0.7 all-gather.2.cloned.1.call-update
  7.9 0.7 fusion.64
  8.6 0.6 reduce-window.6
  9.2 0.2 slice_reduce_fusion
  9.4 0.8 fusion.63
  10.2 0.7 compare_select_fusion.1
  10.9 1.6 scatter_custom_fusion
  12.4 0.7 all_to_all.9
  13.1 10.0 %all-to-all-start = ((s32[16,1,32]{2,1,0:T(1,128)}), s32[16,1,32]{2,1,0:T(1,128)S(1)}, u32[]{:S(2)}, u32[]{:S(2)}) async-start(s32[16,1,32]{2,1,0:T(1,128)} %all_to_all.9), calls=%async_computation | async-start | bytes 16384 | tf_op jit(solution)/shard_map/all_to_all | solution.py:72
  23.8 0.7 compare_and_fusion
  24.5 66.3 %all-gather.2.cloned.1.call-done = bf16[12288,512]{1,0:T(8,128)(2,1)} async-done(((bf16[768,512]{1,0:T(8,128)(2,1)}), bf16[12288,512]{1,0:T(8,128)(2,1)}) %all-gather.2.cloned.1.call-update) | async-done | bytes 12582928 | tf_op jit(solution)/shard_map/all_gather | solution.py:76
  90.8 7.4 %gather_fusion = bf16[256,512]{1,0:T(8,128)(2,1)S(1)} fusion(bf16[12288,512]{1,0:T(8,128)(2,1)} %all-gather.2.cloned.1.call-done, s32[1024]{0:T(1024)S(1)} %pad_clamp_fusion), kind=kCustom, calls=%fused_computation | custom fusion | bytes 525312 | tf_op jit(solution)/shard_map/gather | solution.py:78
  98.2 0.2 convert_reduce_fusion
  98.4 0.2 fusion.38
  98.6 0.0 copy-done
  98.7 2.8 fusion.76
  101.5 0.8 slice_bitcast_fusion
  102.2 0.1 copy.40
  102.4 0.0 copy-start.4
  102.4 0.1 copy.41
  102.5 0.0 copy-start.6
  102.5 0.0 copy-start.8
  102.5 1.6 divide_convert_fusion
  104.1 0.0 copy-done.4
  104.1 0.0 copy-done.6
  104.1 0.0 copy-done.8
  104.1 0.3 fusion.78
  104.5 0.1 fusion.40
  104.6 0.3 copy-done.2
  104.9 0.2 copy.35
  105.1 1.7 multiply_reduce_fusion.1
  106.9 2.1 fusion.75
  108.9 0.1 broadcast_add_fusion
  109.0 0.1 copy.36
  109.2 0.0 copy-start.5
  109.2 2.0 fusion.26
  111.3 0.2 fusion.80
  111.5 0.0 copy-done.7
  111.5 1.0 fusion.79
  112.5 0.9 fusion.81
  113.5 0.1 copy.37
  113.6 1.8 copy.38
  115.4 1.8 copy.39
  117.2 3.4 multiply_reduce_fusion
  120.6 1.0 fusion.74
  121.6 2.9 scatter_custom_fusion.1
  124.5 0.0 all-to-all-done
  124.5 6.9 %all-to-all-start.1 = ((bf16[16,32,512]{2,1,0:T(8,128)(2,1)}), bf16[16,32,512]{2,1,0:T(8,128)(2,1)}, u32[]{:S(2)}, u32[]{:S(2)}) async-start(bf16[16,32,512]{2,1,0:T(8,128)(2,1)} %bitcast.120), calls=%async_computation.1 | async-start | bytes 1048576 | tf_op jit(solution)/shard_map/all_to_all | solution.py:94
  131.4 0.2 all-reduce.9.cloned.1.call-start
  131.6 2.5 fusion.45
  134.1 0.0 all-reduce.9.cloned.1.call-update
  134.1 0.0 all-reduce.7.cloned.1.call-start
  134.2 0.5 broadcast.379
  134.7 0.7 reduce.15
  135.4 0.1 reshape.502
  135.4 10.4 %all-to-all-done.1 = bf16[16,32,512]{2,1,0:T(8,128)(2,1)} async-done(((bf16[16,32,512]{2,1,0:T(8,128)(2,1)}), bf16[16,32,512]{2,1,0:T(8,128)(2,1)}, u32[]{:S(2)}, u32[]{:S(2)}) %all-to-all-start.1) | async-done | bytes 524320 | tf_op jit(solution)/shard_map/all_to_all | solution.py:94
  145.8 5.5 scatter_custom_fusion.2
  151.3 0.0 all-reduce.7.cloned.1.call-update
  151.3 258.6 %all-reduce.9.cloned.1.call-done = f32[512,512]{1,0:T(8,128)} async-done(((f32[512,512]{1,0:T(8,128)}), f32[512,512]{1,0:T(8,128)}) %all-reduce.9.cloned.1.call-update) | async-done | bytes 1048592 | tf_op jit(solution)/shard_map/psum | solution.py:109
  409.9 2.1 multiply_convert_fusion
  412.0 161.6 %all-reduce.7.cloned.1.call-done = f32[768,512]{1,0:T(8,128)} async-done(((f32[768,512]{1,0:T(8,128)}), f32[768,512]{1,0:T(8,128)}) %all-reduce.7.cloned.1.call-update) | async-done | bytes 1572880 | tf_op jit(solution)/shard_map/psum | solution.py:108
  573.7 2.7 copy.58
  (20 shorter events, 0.2 us)
Async XLA Ops:
  7.2 91.5 %copy-start = (bf16[512,2048]{1,0:T(8,128)(2,1)S(1)}, bf16[512,2048]{1,0:T(8,128)(2,1)}, u32[]{:S(2)}) copy-start(bf16[512,2048]{1,0:T(8,128)(2,1)} %param.11) | copy-start | bytes 6291460
  7.2 83.6 %all-gather.2.cloned.1.call-start = ((), (), s32[]{:S(2)}) async-start(), calls=%async_computation.2 | async-start | bytes 13369344 | tf_op jit(solution)/shard_map/all_gather | solution.py:76
  13.1 111.4 %all-to-all-start = ((s32[16,1,32]{2,1,0:T(1,128)}), s32[16,1,32]{2,1,0:T(1,128)S(1)}, u32[]{:S(2)}, u32[]{:S(2)}) async-start(s32[16,1,32]{2,1,0:T(1,128)} %all_to_all.9), calls=%async_computation | async-start | bytes 16384 | tf_op jit(solution)/shard_map/all_to_all | solution.py:72
  102.4 1.8 copy-start.4
  102.5 1.6 copy-start.6
  102.5 1.6 copy-start.8
  104.1 0.8 copy-start.2
  109.2 2.1 copy-start.5
  109.2 2.3 copy-start.7
  111.2 1.3 copy-start.3
  117.2 4.4 copy-start.1
  124.5 21.3 %all-to-all-start.1 = ((bf16[16,32,512]{2,1,0:T(8,128)(2,1)}), bf16[16,32,512]{2,1,0:T(8,128)(2,1)}, u32[]{:S(2)}, u32[]{:S(2)}) async-start(bf16[16,32,512]{2,1,0:T(8,128)(2,1)} %bitcast.120), calls=%async_computation.1 | async-start | bytes 1048576 | tf_op jit(solution)/shard_map/all_to_all | solution.py:94
  131.4 278.5 %all-reduce.9.cloned.1.call-start = ((), (), s32[]{:S(2)}) async-start(), calls=%async_computation.4 | async-start | bytes 2097152 | tf_op jit(solution)/shard_map/psum | solution.py:109
  134.1 439.6 %all-reduce.7.cloned.1.call-start = ((), (), s32[]{:S(2)}) async-start(), calls=%async_computation.3 | async-start | bytes 3145728 | tf_op jit(solution)/shard_map/psum | solution.py:108
Sparse Core Ops, SparseCore 0:
  10.1 80.5 all-gather.1
  137.3 272.5 all-reduce.8
  414.3 159.3 all-reduce.6
where the time goes:
time: 584 us; the launch traced here: 583 us
  waiting for transfers between devices  498 us (85%)
  local copies, waits for them, and re-layouts  18.5 us (3%)
  other arithmetic  18.5 us (3%)
  starting transfers between devices  17.1 us (3%)
  matrix products  16.5 us (3%)
  between operations  14.6 us (2%)
    psum x1, waiting for transfers between devices, per_device(): dense_total = lax.psum(dense_part, ('dp', 'table'))  259 us
    psum x1, waiting for transfers between devices, per_device(): table_grad = lax.psum(local_grad, 'dp')  162 us
    all_gather x1, waiting for transfers between devices, per_device(): piece = lax.all_gather(table, 'table', axis=0, tiled=True)  66.3 us
  transfers between devices with their start and end apart: 5, of which 4 were waited for; matrix products, arithmetic and copies ran while one was open for 9% of the time, Pallas kernels for 0%

commit v1 on v0

--- a/solution.py
+++ b/solution.py
@@ -106,7 +106,7 @@
     total_slots = slot_count * lax.axis_size("dp") * groups
     grad_scale = 1.0 / math.sqrt(total_slots)
     table_grad = lax.psum(local_grad, "dp")
-    dense_total = lax.psum(dense_part, ("dp", "table"))
+    dense_total = lax.psum(lax.psum(dense_part, "table"), "dp")
     dense_grad = (dense_total * grad_scale).astype(jnp.bfloat16)
     return (table_grad, dense_grad)
 

time: 584 us -> 435 us (0.74)
  the two profiles are of different devices: /device:TPU:64 before, /device:TPU:2 now
where the time goes in v1:
time: 435 us; the launch traced here: 434 us
  waiting for transfers between devices  352 us (81%)
  other arithmetic  18.5 us (4%)
  local copies, waits for them, and re-layouts  17 us (4%)
  matrix products  16.5 us (4%)
  starting transfers between devices  15 us (3%)
  between operations  14.6 us (3%)
    psum x1, waiting for transfers between devices, per_device(): table_grad = lax.psum(local_grad, 'dp')  170 us
    psum x1, waiting for transfers between devices, per_device(): dense_total = lax.psum(lax.psum(dense_part, 'table'), 'dp')  100 us
    all_gather x1, waiting for transfers between devices, per_device(): piece = lax.all_gather(table, 'table', axis=0, tiled=True)  68.9 us
    all_to_all x1, waiting for transfers between devices, per_device(): lax.all_to_all(outgoing.reshape(groups, capacity, model_width), 'table',...  12 us
    all_to_all x1, starting transfers between devices, per_device(): lax.all_to_all(requested, 'table', split_axis=0, concat_axis=0, tiled=True)  10.4 us
  transfers between devices with their start and end apart: 5, of which 4 were waited for; matrix products, arithmetic and copies ran while one was open for 11% of the time, Pallas kernels for 0%

profile of v1, /device:TPU:2, one launch (start us, length us, event | category | flops | bytes accessed | tf_op | source)
XLA Modules:
  0.0 434.1 jit_solution(14185518587502341418)
XLA Ops:
  7.2 0.0 copy-start
  7.2 0.0 all-gather.2.cloned.1.call-start
  7.2 0.7 all-gather.2.cloned.1.call-update
  7.9 0.7 fusion.64
  8.6 0.6 reduce-window.6
  9.2 0.2 slice_reduce_fusion
  9.4 0.8 fusion.63
  10.2 0.7 compare_select_fusion.1
  10.9 1.6 scatter_custom_fusion
  12.4 0.7 all_to_all.9
  13.1 10.4 %all-to-all-start = ((s32[16,1,32]{2,1,0:T(1,128)}), s32[16,1,32]{2,1,0:T(1,128)S(1)}, u32[]{:S(2)}, u32[]{:S(2)}) async-start(s32[16,1,32]{2,1,0:T(1,128)} %all_to_all.9), calls=%async_computation | async-start | bytes 16384 | tf_op jit(solution)/shard_map/all_to_all | solution.py:72
  24.2 0.7 compare_and_fusion
  25.0 68.9 %all-gather.2.cloned.1.call-done = bf16[12288,512]{1,0:T(8,128)(2,1)} async-done(((bf16[768,512]{1,0:T(8,128)(2,1)}), bf16[12288,512]{1,0:T(8,128)(2,1)}) %all-gather.2.cloned.1.call-update) | async-done | bytes 12582928 | tf_op jit(solution)/shard_map/all_gather | solution.py:76
  93.9 7.4 %gather_fusion = bf16[256,512]{1,0:T(8,128)(2,1)S(1)} fusion(bf16[12288,512]{1,0:T(8,128)(2,1)} %all-gather.2.cloned.1.call-done, s32[1024]{0:T(1024)S(1)} %pad_clamp_fusion), kind=kCustom, calls=%fused_computation | custom fusion | bytes 525312 | tf_op jit(solution)/shard_map/gather | solution.py:78
  101.3 0.2 convert_reduce_fusion
  101.5 0.2 fusion.38
  101.8 0.0 copy-done
  101.8 2.8 fusion.76
  104.6 0.8 slice_bitcast_fusion
  105.4 0.1 copy.40
  105.5 0.0 copy-start.5
  105.5 0.1 copy.41
  105.7 0.0 copy-start.7
  105.7 0.0 copy-start.9
  105.7 1.6 divide_convert_fusion
  107.2 0.0 copy-done.5
  107.3 0.0 copy-done.7
  107.3 0.3 fusion.78
  107.6 0.1 fusion.40
  107.7 0.3 copy-done.2
  108.0 0.2 copy.35
  108.3 1.7 multiply_reduce_fusion.1
  110.0 2.1 fusion.75
  112.0 0.1 broadcast_add_fusion
  112.2 0.1 copy.36
  112.3 2.0 fusion.26
  114.4 0.2 fusion.80
  114.6 0.0 copy-done.8
  114.6 1.0 fusion.79
  115.6 0.0 copy-done.3
  115.6 0.9 fusion.81
  116.6 0.1 copy.37
  116.7 1.8 copy.38
  118.5 1.8 copy.39
  120.3 3.4 multiply_reduce_fusion
  123.7 1.0 fusion.74
  124.7 0.0 copy-done.1
  124.7 2.9 scatter_custom_fusion.1
  127.6 0.0 all-to-all-done
  127.6 4.2 all-to-all-start.1
  131.9 0.2 all-reduce.8.cloned.1.call-start
  132.1 2.5 fusion.45
  134.6 0.0 all-reduce.8.cloned.1.call-update
  134.6 0.0 all-reduce.10.cloned.1.call-start
  134.7 0.5 broadcast.379
  135.2 0.7 reduce.15
  135.9 0.1 reshape.502
  136.0 12.0 %all-to-all-done.1 = bf16[16,32,512]{2,1,0:T(8,128)(2,1)} async-done(((bf16[16,32,512]{2,1,0:T(8,128)(2,1)}), bf16[16,32,512]{2,1,0:T(8,128)(2,1)}, u32[]{:S(2)}, u32[]{:S(2)}) %all-to-all-start.1) | async-done | bytes 524320 | tf_op jit(solution)/shard_map/all_to_all | solution.py:94
  147.9 5.4 %scatter_custom_fusion.2 = f32[768,512]{1,0:T(8,128)} fusion(s32[512]{0:T(512)S(1)} %bitcast.137, bf16[512,512]{1,0:T(8,128)(2,1)} %bitcast.42, f32[]{:T(128)} %constant.15.clone.1), kind=kCustom, calls=%fused_computation.35 | custom fusion | flops 524288 | bytes 2097156 | tf_op jit(solution)/shard_map/scatter-add | solution.py:104
  153.3 100.4 %all-reduce.8.cloned.1.call-done = f32[512,512]{1,0:T(8,128)} async-done(((f32[512,512]{1,0:T(8,128)}), f32[512,512]{1,0:T(8,128)}) %all-reduce.8.cloned.1.call-update) | async-done | bytes 1048592 | tf_op jit(solution)/shard_map/psum | solution.py:109
  253.7 0.0 all-reduce.10.cloned.1.call-update
  253.7 170.5 %all-reduce.10.cloned.1.call-done = (f32[768,512]{1,0:T(8,128)}, f32[512,512]{1,0:T(8,128)}) async-done(((f32[768,512]{1,0:T(8,128)}, f32[512,512]{1,0:T(8,128)}), (f32[768,512]{1,0:T(8,128)}, f32[512,512]{1,0:T(8,128)})) %all-reduce.10.cloned.1.call-update) | async-done | bytes 2621456 | tf_op jit(solution)/shard_map/psum | solution.py:108
  424.2 2.3 multiply_convert_fusion
  426.4 1.1 copy.59
  (22 shorter events, 0.2 us)
Async XLA Ops:
  7.2 94.6 %copy-start = (bf16[512,2048]{1,0:T(8,128)(2,1)S(1)}, bf16[512,2048]{1,0:T(8,128)(2,1)}, u32[]{:S(2)}) copy-start(bf16[512,2048]{1,0:T(8,128)(2,1)} %param.11) | copy-start | bytes 6291460
  7.2 86.7 %all-gather.2.cloned.1.call-start = ((), (), s32[]{:S(2)}) async-start(), calls=%async_computation.2 | async-start | bytes 13369344 | tf_op jit(solution)/shard_map/all_gather | solution.py:76
  13.1 114.5 %all-to-all-start = ((s32[16,1,32]{2,1,0:T(1,128)}), s32[16,1,32]{2,1,0:T(1,128)S(1)}, u32[]{:S(2)}, u32[]{:S(2)}) async-start(s32[16,1,32]{2,1,0:T(1,128)} %all_to_all.9), calls=%async_computation | async-start | bytes 16384 | tf_op jit(solution)/shard_map/all_to_all | solution.py:72
  105.5 1.7 copy-start.5
  105.7 1.6 copy-start.7
  105.7 1.6 copy-start.9
  107.3 0.8 copy-start.2
  112.3 2.1 copy-start.6
  112.3 2.3 copy-start.8
  114.4 1.3 copy-start.3
  120.3 4.4 %copy-start.1 = (bf16[1,256,512]{2,1,0:T(8,128)(2,1)S(1)}, bf16[1,256,512]{2,1,0:T(8,128)(2,1)}, u32[]{:S(2)}) copy-start(bf16[1,256,512]{2,1,0:T(8,128)(2,1)} %param.13) | copy-start | bytes 786436
  127.6 20.3 %all-to-all-start.1 = ((bf16[16,32,512]{2,1,0:T(8,128)(2,1)}), bf16[16,32,512]{2,1,0:T(8,128)(2,1)}, u32[]{:S(2)}, u32[]{:S(2)}) async-start(bf16[16,32,512]{2,1,0:T(8,128)(2,1)} %bitcast.120), calls=%async_computation.1 | async-start | bytes 1048576 | tf_op jit(solution)/shard_map/all_to_all | solution.py:94
  131.9 121.8 %all-reduce.8.cloned.1.call-start = ((), (), s32[]{:S(2)}) async-start(), calls=%async_computation.3 | async-start | bytes 2097152 | tf_op jit(solution)/shard_map/psum | solution.py:109
  134.6 289.5 %all-reduce.10.cloned.1.call-start = ((), (), s32[]{:S(2)}) async-start(), calls=%async_computation.4 | async-start | bytes 5242880 | tf_op jit(solution)/shard_map/psum | solution.py:108
  424.2 2.3 copy-start.4
Sparse Core Ops, SparseCore 0:
  10.1 83.7 all-gather.1
  135.1 118.5 all-reduce.7
  258.4 165.7 all-reduce.9
